TPU v7x, 32 devices: a whole 2x2x4 slice. The times are simulated.
32 devices in a mesh: rows: 4 (over x, core), feat: 8 (over z, y).
Axes of the slice: x: 2, y: 2, z: 4, core: 2. Of those that a mesh axis runs over, the one named last changes fastest.
Arguments:
- embeddings: bfloat16 [512, 1024], P(('rows', 'feat')), may hold values from -12 to 12
- freqs: bfloat16 [1024, 65536], P(None, 'feat'), may hold values from -0.1875 to 0.1875
- phases: float32 [65536], P('feat'), may hold values from 0 to 6.2831855
- sketch: bfloat16 [65536, 256], P('feat'), may hold values from -0.0234375 to 0.0234375
Outputs:
- basis: float32 [512, 256], P(('rows', 'feat'))
- coeffs: float32 [256, 65536], P(None, 'feat')
All inputs are finite; a program needn't handle non-finite values.
Results may differ from a plain program's by a relative error of at most 0.0048.
Values may be sent and summed in bfloat16 or wider, within the bound.
A program may use at most 128 MiB of HBM per device.

v0:
```python
import jax
import jax.numpy as jnp
from jax import lax
from jax.sharding import PartitionSpec as P


def per_device(embeddings, freqs, phases, sketch):
    rows_dev = embeddings.shape[0]
    row_count = rows_dev * lax.axis_size("feat") * lax.axis_size("rows")
    mixed = jnp.dot(
        lax.all_gather(embeddings, "feat", axis=0, tiled=True),
        freqs,
        preferred_element_type=jnp.float32,
    )
    features = jnp.cos(mixed + phases).astype(jnp.bfloat16)
    owned_rows = lax.psum_scatter(
        jnp.dot(features, sketch, preferred_element_type=jnp.float32),
        "feat",
        scatter_dimension=0,
        tiled=True,
    )
    local_gram = jnp.dot(owned_rows.T, owned_rows, precision=lax.Precision.HIGHEST)
    gram_matrix = lax.psum(local_gram, ("rows", "feat")) / row_count
    factor = jnp.linalg.cholesky(gram_matrix)
    basis = jax.scipy.linalg.solve_triangular(factor, owned_rows.T, lower=True).T
    block_basis = lax.all_gather(basis.astype(jnp.bfloat16), "feat", axis=0, tiled=True)
    partial_value = lax.dot_general(
        block_basis, features, (((0,), (0,)), ((), ())), preferred_element_type=jnp.float32
    )
    coeffs = lax.psum(partial_value, "rows") / row_count
    return (basis, coeffs)


def solution(mesh):
    placed = (P(("rows", "feat"), None), P(None, "feat"), P("feat"), P("feat", None))
    return jax.shard_map(
        per_device,
        mesh=mesh,
        in_specs=placed,
        out_specs=(P(("rows", "feat"), None), P(None, "feat")),
        check_vma=False,
    )
```

profile of v0, /device:TPU:0, one launch (start us, length us, event | category | flops | bytes accessed | tf_op | source)
XLA Modules:
  0.0 516.5 jit_solution(3243274491165157878)
XLA Ops:
  7.2 0.0 reduce-scatter.2.cloned.1.call-start
  7.2 32.7 %all_gather.6 = bf16[128,1024]{1,0:T(8,128)(2,1)S(1)} all-gather(bf16[16,1024]{1,0:T(8,128)(2,1)} %param.4), channel_id=1, replica_groups=mesh['rows'=4,'feat'=8] {'feat'}, dimensions={0}, use_global_device_ids=true | all-gather | bytes 294912 | tf_op jit(solution)/shard_map/all_gather | solution.py:11
  39.9 0.0 copy-start
  40.0 18.1 %fusion.1 = bf16[128,8192]{1,0:T(8,128)(2,1)S(1)} fusion(bf16[128,1024]{1,0:T(8,128)(2,1)S(1)} %all_gather.6, bf16[1024,8192]{1,0:T(8,128)(2,1)} %param.5, f32[8192]{0:T(1024)} %param.6), kind=kOutput, calls=%fused_computation.4 | convolution fusion | flops 2149580800 | bytes 19169280 | tf_op jit(solution)/shard_map/dot_general | solution.py:10
  58.1 0.0 copy-done
  58.1 1.5 fusion.12
  59.6 0.0 reduce-scatter.2.cloned.1.call-update
  59.6 0.0 all-reduce.4.cloned.1.call-start
  59.6 62.0 %reduce-scatter.2.cloned.1.call-done = f32[16,256]{1,0:T(8,128)} async-done(((f32[128,256]{1,0:T(8,128)}), f32[16,256]{1,0:T(8,128)}) %reduce-scatter.2.cloned.1.call-update) | async-done | bytes 16400 | tf_op jit(solution)/shard_map/reduce_scatter | solution.py:16
  121.6 0.0 copy-start.1
  121.6 1.9 fusion.13
  123.6 0.0 all-reduce.4.cloned.1.call-update
  123.6 0.2 all-reduce.6.cloned.1.call-start
  123.8 128.0 %all-reduce.4.cloned.1.call-done = f32[256,256]{0,1:T(8,128)} async-done(((f32[256,256]{0,1:T(8,128)}), f32[256,256]{0,1:T(8,128)}) %all-reduce.4.cloned.1.call-update) | async-done | bytes 262160 | tf_op jit(solution)/shard_map/psum | solution.py:23
  251.8 1.0 broadcast_multiply_fusion.1
  252.8 0.1 copy.7
  252.9 1.0 fusion.2
  253.9 11.7 %cholesky.50 = f32[128,128]{1,0:T(8,128)S(1)} custom-call(f32[128,128]{1,0:T(8,128)S(1)} %cholesky.118), custom_call_target="Cholesky" | custom-call | tf_op jit(solution)/shard_map/jit(cholesky)/cholesky | solution.py:24
  265.7 9.8 %custom-call.15 = f32[1,128,128]{1,2,0:T(8,128)S(1)} custom-call(f32[1,128,128]{2,1,0:T(8,128)S(1)} %get-tuple-element.25), custom_call_target="InvertDiagBlocksLowerTriangular" | custom-call | tf_op jit(solution)/shard_map/jit(cholesky)/cholesky | solution.py:24
  275.5 0.2 constant_dynamic-update-slice_fusion.1
  275.7 0.3 convolution_subtract_fusion
  276.0 11.7 %cholesky.105 = f32[128,128]{1,0:T(8,128)S(1)} custom-call(f32[128,128]{1,0:T(8,128)S(1)} %convolution_subtract_fusion), custom_call_target="Cholesky" | custom-call | tf_op jit(solution)/shard_map/jit(cholesky)/cholesky | solution.py:24
  287.8 0.7 compare_reduce_fusion
  289.9 0.1 triangular_solve.57
  289.9 4.3 while.1
  290.1 0.6 fusion.28
  290.7 1.4 bitcast_dynamic-update-slice_fusion.2
  292.2 0.6 fusion.28
  292.8 1.4 bitcast_dynamic-update-slice_fusion.2
  294.2 19.7 %custom-call.16 = f32[2,128,128]{1,2,0:T(8,128)S(1)} custom-call(f32[2,128,128]{2,1,0:T(8,128)S(1)} %get-tuple-element.9), custom_call_target="InvertDiagBlocksLowerTriangular" | custom-call | tf_op jit(solution)/shard_map/jit(_solve_triangular)/triangular_solve | solution.py:25
  313.9 0.0 copy-done.1
  313.9 0.2 fusion.5
  314.1 0.2 convolution_subtract_fusion.1
  314.3 0.2 fusion.4
  314.5 0.6 fusion.10
  315.1 30.5 %all_gather.7 = bf16[128,256]{1,0:T(8,128)(2,1)S(1)} all-gather(bf16[16,256]{1,0:T(8,128)(2,1)S(1)} %get-tuple-element.18), channel_id=1, replica_groups=mesh['rows'=4,'feat'=8] {'feat'}, dimensions={0}, use_global_device_ids=true | all-gather | bytes 73728 | tf_op jit(solution)/shard_map/all_gather | solution.py:26
  345.6 4.7 fusion.14
  350.3 0.0 all-reduce.6.cloned.1.call-update
  350.3 152.0 %all-reduce.6.cloned.1.call-done = f32[256,8192]{1,0:T(8,128)} async-done(((f32[256,8192]{1,0:T(8,128)}), f32[256,8192]{1,0:T(8,128)}) %all-reduce.6.cloned.1.call-update) | async-done | bytes 8388624 | tf_op jit(solution)/shard_map/psum | solution.py:30
  502.3 7.7 %broadcast_multiply_fusion = f32[256,8192]{1,0:T(8,128)} fusion(f32[256,8192]{1,0:T(8,128)} %all-reduce.6.cloned.1.call-done), kind=kLoop, calls=%fused_computation.5 | loop fusion | flops 2097152 | bytes 16777216 | tf_op jit(solution)/shard_map/div | solution.py:30
  (9 shorter events, 0.1 us)
Async XLA Ops:
  7.2 114.5 %reduce-scatter.2.cloned.1.call-start = ((), (), s32[]{:S(2)}) async-start(), calls=%async_computation.1 | async-start | bytes 147456 | tf_op jit(solution)/shard_map/reduce_scatter | solution.py:16
  39.9 18.2 %copy-start = (bf16[8192,256]{1,0:T(8,128)(2,1)S(1)}, bf16[8192,256]{1,0:T(8,128)(2,1)}, u32[]{:S(2)}) copy-start(bf16[8192,256]{1,0:T(8,128)(2,1)} %param.7) | copy-start | bytes 12582916
  59.6 192.2 %all-reduce.4.cloned.1.call-start = ((), (), s32[]{:S(2)}) async-start(), calls=%async_computation.2 | async-start | bytes 524288 | tf_op jit(solution)/shard_map/psum | solution.py:23
  121.6 192.3 %copy-start.1 = (f32[16,256]{1,0:T(8,128)S(1)}, f32[16,256]{1,0:T(8,128)}, u32[]{:S(2)}) copy-start(f32[16,256]{1,0:T(8,128)} %reduce-scatter.2.cloned.1.call-done) | copy-start | bytes 49156
  123.6 378.7 %all-reduce.6.cloned.1.call-start = ((), (), s32[]{:S(2)}) async-start(), calls=%async_computation.3 | async-start | bytes 16777216 | tf_op jit(solution)/shard_map/psum | solution.py:30
Sparse Core Ops, SparseCore 0:
  59.7 61.8 reduce-scatter.1
  127.7 124.0 all-reduce.3
  350.4 151.8 all-reduce.5
where the time goes:
time: 517 us
  waiting for transfers between devices  342 us (66%)
  other arithmetic  64 us (12%)
  blocking collectives  63.2 us (12%)
  matrix products  27.2 us (5%)
  between operations  15.2 us (3%)
    psum x1, waiting for transfers between devices, per_device(): coeffs = lax.psum(partial_value, 'rows') / row_count  152 us
    psum x1, waiting for transfers between devices, per_device(): gram_matrix = lax.psum(local_gram, ('rows', 'feat')) / row_count  128 us
    reduce_scatter x1, waiting for transfers between devices, per_device(): lax.psum_scatter(jnp.dot(features, sketch, preferred_element_type=jnp.flo...  62 us
    another operation x6, other arithmetic, per_device(): factor = jnp.linalg.cholesky(gram_matrix)  34 us
    all_gather x1, blocking collectives, per_device(): lax.all_gather(embeddings, 'feat', axis=0, tiled=True)  32.7 us
    all_gather x1, blocking collectives, per_device(): lax.all_gather(basis.astype(jnp.bfloat16), 'feat', axis=0, tiled=True)  30.5 us
    another operation x3, other arithmetic, per_device(): jax.scipy.linalg.solve_triangular(factor, owned_rows.T, lower=True)  19.7 us
    dot_general x1, matrix products, per_device(): jnp.dot(lax.all_gather(embeddings, 'feat', axis=0, tiled=True), freqs, pr...  18.1 us
  transfers between devices with their start and end apart: 3, of which 3 were waited for; matrix products, arithmetic and copies ran while one was open for 0% of the time, Pallas kernels for 0%

commit v1 on v0

--- a/solution.py
+++ b/solution.py
@@ -2,6 +2,10 @@
 import jax.numpy as jnp
 from jax import lax
 from jax.sharding import PartitionSpec as P
+
+
+def begin_the_members_all(array_here, bus_axis, dev_axis):
+    return lax.psum(lax.psum(array_here, bus_axis), dev_axis)
 
 
 def per_device(embeddings, freqs, phases, sketch):
@@ -20,7 +24,7 @@
         tiled=True,
     )
     local_gram = jnp.dot(owned_rows.T, owned_rows, precision=lax.Precision.HIGHEST)
-    gram_matrix = lax.psum(local_gram, ("rows", "feat")) / row_count
+    gram_matrix = begin_the_members_all(local_gram, "feat", "rows") / row_count
     factor = jnp.linalg.cholesky(gram_matrix)
     basis = jax.scipy.linalg.solve_triangular(factor, owned_rows.T, lower=True).T
     block_basis = lax.all_gather(basis.astype(jnp.bfloat16), "feat", axis=0, tiled=True)

time: 517 us -> 495 us (0.957)
  waiting for transfers between devices: 342 us -> 320 us
    psum x1 -> x2, waiting for transfers between devices: 128 us -> 105 us  [begin_the_members_all(): return lax.psum(lax.psum(array_here, bus_axis), dev_axis)]
  transfers between devices with their start and end apart: 3 -> 4, of which waited for: 3 -> 4; matrix products, arithmetic and copies ran while one was open for 0% -> 0% of each run, Pallas kernels for 0% -> 0%
where the time goes in v1:
time: 495 us
  waiting for transfers between devices  320 us (65%)
  other arithmetic  64 us (13%)
  blocking collectives  63.3 us (13%)
  matrix products  27.2 us (5%)
  between operations  15.2 us (3%)
    psum x1, waiting for transfers between devices, per_device(): coeffs = lax.psum(partial_value, 'rows') / row_count  153 us
    psum x2, waiting for transfers between devices, begin_the_members_all(): return lax.psum(lax.psum(array_here, bus_axis), dev_axis)  105 us
    reduce_scatter x1, waiting for transfers between devices, per_device(): lax.psum_scatter(jnp.dot(features, sketch, preferred_element_type=jnp.flo...  62 us
    another operation x6, other arithmetic, per_device(): factor = jnp.linalg.cholesky(gram_matrix)  34 us
    all_gather x1, blocking collectives, per_device(): lax.all_gather(embeddings, 'feat', axis=0, tiled=True)  32.7 us
    all_gather x1, blocking collectives, per_device(): lax.all_gather(basis.astype(jnp.bfloat16), 'feat', axis=0, tiled=True)  30.6 us
    another operation x3, other arithmetic, per_device(): jax.scipy.linalg.solve_triangular(factor, owned_rows.T, lower=True)  19.7 us
    dot_general x1, matrix products, per_device(): jnp.dot(lax.all_gather(embeddings, 'feat', axis=0, tiled=True), freqs, pr...  18.1 us
  transfers between devices with their start and end apart: 4, of which 4 were waited for; matrix products, arithmetic and copies ran while one was open for 0% of the time, Pallas kernels for 0%

profile of v1, /device:TPU:0, one launch (start us, length us, event | category | flops | bytes accessed | tf_op | source)
XLA Modules:
  0.0 494.6 jit_solution(12629000864545139548)
XLA Ops:
  7.2 0.0 reduce-scatter.2.cloned.1.call-start
  7.2 32.7 %all_gather.6 = bf16[128,1024]{1,0:T(8,128)(2,1)S(1)} all-gather(bf16[16,1024]{1,0:T(8,128)(2,1)} %param.4), channel_id=1, replica_groups=mesh['rows'=4,'feat'=8] {'feat'}, dimensions={0}, use_global_device_ids=true | all-gather | bytes 294912 | tf_op jit(solution)/shard_map/all_gather | solution.py:15
  39.9 0.0 copy-start
  40.0 18.1 %fusion.1 = bf16[128,8192]{1,0:T(8,128)(2,1)S(1)} fusion(bf16[128,1024]{1,0:T(8,128)(2,1)S(1)} %all_gather.6, bf16[1024,8192]{1,0:T(8,128)(2,1)} %param.5, f32[8192]{0:T(1024)} %param.6), kind=kOutput, calls=%fused_computation.4 | convolution fusion | flops 2149580800 | bytes 19169280 | tf_op jit(solution)/shard_map/dot_general | solution.py:14
  58.1 0.0 copy-done
  58.1 1.5 fusion.12
  59.6 0.0 reduce-scatter.2.cloned.1.call-update
  59.6 0.0 all-reduce.5.cloned.1.call-start
  59.6 62.0 %reduce-scatter.2.cloned.1.call-done = f32[16,256]{1,0:T(8,128)} async-done(((f32[128,256]{1,0:T(8,128)}), f32[16,256]{1,0:T(8,128)}) %reduce-scatter.2.cloned.1.call-update) | async-done | bytes 16400 | tf_op jit(solution)/shard_map/reduce_scatter | solution.py:20
  121.6 0.0 copy-start.1
  121.6 1.9 fusion.13
  123.6 0.0 all-reduce.5.cloned.1.call-update
  123.6 0.0 all-reduce.7.cloned.1.call-start
  123.6 71.5 %all-reduce.5.cloned.1.call-done = f32[256,256]{0,1:T(8,128)} async-done(((f32[256,256]{0,1:T(8,128)}), f32[256,256]{0,1:T(8,128)}) %all-reduce.5.cloned.1.call-update) | async-done | bytes 262160 | tf_op jit(solution)/shard_map/psum | solution.py:8
  195.2 0.0 all-reduce.7.cloned.1.call-update
  195.2 0.2 all-reduce.9.cloned.1.call-start
  195.4 33.5 %all-reduce.7.cloned.1.call-done = f32[256,256]{0,1:T(8,128)} async-done(((f32[256,256]{0,1:T(8,128)}), f32[256,256]{0,1:T(8,128)}) %all-reduce.7.cloned.1.call-update) | async-done | bytes 262160 | tf_op jit(solution)/shard_map/psum | solution.py:8
  228.9 1.0 broadcast_multiply_fusion.1
  229.9 0.1 copy.7
  230.0 1.0 fusion.2
  231.0 11.7 %cholesky.50 = f32[128,128]{1,0:T(8,128)S(1)} custom-call(f32[128,128]{1,0:T(8,128)S(1)} %cholesky.118), custom_call_target="Cholesky" | custom-call | tf_op jit(solution)/shard_map/jit(cholesky)/cholesky | solution.py:28
  242.8 9.8 %custom-call.15 = f32[1,128,128]{1,2,0:T(8,128)S(1)} custom-call(f32[1,128,128]{2,1,0:T(8,128)S(1)} %get-tuple-element.25), custom_call_target="InvertDiagBlocksLowerTriangular" | custom-call | tf_op jit(solution)/shard_map/jit(cholesky)/cholesky | solution.py:28
  252.6 0.2 constant_dynamic-update-slice_fusion.1
  252.8 0.3 convolution_subtract_fusion
  253.1 11.7 %cholesky.105 = f32[128,128]{1,0:T(8,128)S(1)} custom-call(f32[128,128]{1,0:T(8,128)S(1)} %convolution_subtract_fusion), custom_call_target="Cholesky" | custom-call | tf_op jit(solution)/shard_map/jit(cholesky)/cholesky | solution.py:28
  264.8 0.7 compare_reduce_fusion
  266.9 0.1 triangular_solve.57
  267.0 4.3 while.1
  267.2 0.6 fusion.28
  267.8 1.4 bitcast_dynamic-update-slice_fusion.2
  269.3 0.6 fusion.28
  269.9 1.4 bitcast_dynamic-update-slice_fusion.2
  271.3 19.7 %custom-call.16 = f32[2,128,128]{1,2,0:T(8,128)S(1)} custom-call(f32[2,128,128]{2,1,0:T(8,128)S(1)} %get-tuple-element.9), custom_call_target="InvertDiagBlocksLowerTriangular" | custom-call | tf_op jit(solution)/shard_map/jit(_solve_triangular)/triangular_solve | solution.py:29
  291.0 0.0 copy-done.1
  291.0 0.2 fusion.5
  291.1 0.2 convolution_subtract_fusion.1
  291.3 0.2 fusion.4
  291.5 0.6 fusion.10
  292.2 30.6 %all_gather.7 = bf16[128,256]{1,0:T(8,128)(2,1)S(1)} all-gather(bf16[16,256]{1,0:T(8,128)(2,1)S(1)} %get-tuple-element.18), channel_id=1, replica_groups=mesh['rows'=4,'feat'=8] {'feat'}, dimensions={0}, use_global_device_ids=true | all-gather | bytes 73728 | tf_op jit(solution)/shard_map/all_gather | solution.py:30
  322.7 4.7 fusion.14
  327.4 0.0 all-reduce.9.cloned.1.call-update
  327.4 153.0 %all-reduce.9.cloned.1.call-done = f32[256,8192]{1,0:T(8,128)} async-done(((f32[256,8192]{1,0:T(8,128)}), f32[256,8192]{1,0:T(8,128)}) %all-reduce.9.cloned.1.call-update) | async-done | bytes 8388624 | tf_op jit(solution)/shard_map/psum | solution.py:34
  480.4 7.7 %broadcast_multiply_fusion = f32[256,8192]{1,0:T(8,128)} fusion(f32[256,8192]{1,0:T(8,128)} %all-reduce.9.cloned.1.call-done), kind=kLoop, calls=%fused_computation.5 | loop fusion | flops 2097152 | bytes 16777216 | tf_op jit(solution)/shard_map/div | solution.py:34
  (9 shorter events, 0.1 us)
Async XLA Ops:
  7.2 114.5 %reduce-scatter.2.cloned.1.call-start = ((), (), s32[]{:S(2)}) async-start(), calls=%async_computation.1 | async-start | bytes 147456 | tf_op jit(solution)/shard_map/reduce_scatter | solution.py:20
  39.9 18.2 %copy-start = (bf16[8192,256]{1,0:T(8,128)(2,1)S(1)}, bf16[8192,256]{1,0:T(8,128)(2,1)}, u32[]{:S(2)}) copy-start(bf16[8192,256]{1,0:T(8,128)(2,1)} %param.7) | copy-start | bytes 12582916
  59.6 135.6 %all-reduce.5.cloned.1.call-start = ((), (), s32[]{:S(2)}) async-start(), calls=%async_computation.2 | async-start | bytes 524288 | tf_op jit(solution)/shard_map/psum | solution.py:8
  121.6 169.4 %copy-start.1 = (f32[16,256]{1,0:T(8,128)S(1)}, f32[16,256]{1,0:T(8,128)}, u32[]{:S(2)}) copy-start(f32[16,256]{1,0:T(8,128)} %reduce-scatter.2.cloned.1.call-done) | copy-start | bytes 49156
  123.6 105.3 %all-reduce.7.cloned.1.call-start = ((), (), s32[]{:S(2)}) async-start(), calls=%async_computation.3 | async-start | bytes 524288 | tf_op jit(solution)/shard_map/psum | solution.py:8
  195.2 285.2 %all-reduce.9.cloned.1.call-start = ((), (), s32[]{:S(2)}) async-start(), calls=%async_computation.4 | async-start | bytes 16777216 | tf_op jit(solution)/shard_map/psum | solution.py:34
Sparse Core Ops, SparseCore 0:
  59.7 61.8 reduce-scatter.1
  125.5 69.5 all-reduce.4
  197.6 31.2 all-reduce.6
  327.5 152.7 all-reduce.8
